TPU v7x, 32 devices: a whole 2x2x4 slice. The times are simulated.
32 devices in a mesh: subj: 4 (over y, x), slab: 8 (over z, core).
Axes of the slice: x: 2, y: 2, z: 4, core: 2. Of those that a mesh axis runs over, the one named last changes fastest.
Arguments:
- subjects_data: bfloat16 [16384, 16, 512], P('subj', 'slab'), may hold values from -6 to 6
- covariates: bfloat16 [3, 16384], P(None, 'subj'), may hold values from -5 to 5
- permutes: int32 [32, 16384], P(None, 'subj'), may hold values from 0 to 16383, as said below
- brain_mask: int32 [16, 512], P('slab'), may hold values 0 or 1
Outputs:
- smooth_t: float32 [16, 512], P('slab')
- p_values: float32 [16, 512], P('slab')
- perm_peaks: float32 [32], replicated
Inputs may be any that keep to these rules, and one draw needn't show every extreme that they name: `permutes`: each row is a permutation of the subjects that maps every aligned block of 256 subjects onto itself.
All inputs are finite; a program needn't handle non-finite values. No bound on the sum of `brain_mask` on one device may be relied on, other than what follows from the above.
Results may differ from a plain program's by a relative error of at most 0.0003.
Values sent between devices are 32-bit elements; how exact they have to be, the bound alone decides.
A program may use at most 64 MiB of HBM per device.

v0:
```python
import math

import jax
import jax.numpy as jnp
from jax import lax
from jax.sharding import PartitionSpec as P

BLOCK = 256
PX = 16
PY = 32


gauss_raw = tuple((math.exp(-0.5 * (offset - 2) ** 2) for offset in range(5)))
gauss_taps = tuple((value / sum(gauss_raw) for value in gauss_raw))


def padded_2(cells, sides, width):
    for axis, dim in sides:
        count = lax.axis_size(axis)
        ends = count - 1
        head = lax.slice_in_dim(cells, 0, width, axis=dim)
        tail = lax.slice_in_dim(cells, cells.shape[dim] - width, cells.shape[dim], axis=dim)
        cells = jnp.concatenate(
            [
                lax.ppermute(tail, axis, [(i, (i + 1) % count) for i in range(ends)]),
                cells,
                lax.ppermute(head, axis, [((i + 1) % count, i) for i in range(ends)]),
            ],
            axis=dim,
        )
    return cells


def band_weight(gap):
    total = jnp.zeros(gap.shape, jnp.float32)
    for position, weight in enumerate(gauss_taps):
        total = total + weight * (gap == position - 2).astype(jnp.float32)
    return total


def plane_kernel(rows_x, rows_y):
    cell_index = jnp.arange(rows_x * rows_y, dtype=jnp.int32)
    cell_row = cell_index // rows_y
    cell_col = cell_index % rows_y
    row_gap = cell_row[:, None] - cell_row[None, :]
    col_gap = cell_col[:, None] - cell_col[None, :]
    return band_weight(row_gap) * band_weight(col_gap)


def permute_design(permutes, design):
    copies = permutes.shape[0]
    row_count = design.shape[0]
    subj_rows = design.shape[1]
    blocks = subj_rows // BLOCK
    local_idx = (permutes % BLOCK).reshape(copies, blocks, BLOCK).transpose(1, 0, 2)
    block_rows = design.reshape(row_count, blocks, BLOCK).transpose(1, 0, 2)

    def one_block(pair):
        local_part, design_part = pair
        onehot = (
            local_part[:, :, None] == jnp.arange(BLOCK, dtype=jnp.int32)[None, None, :]
        ).astype(jnp.bfloat16)
        return jnp.einsum(
            "ci,pij->pcj", design_part, onehot, preferred_element_type=jnp.float32
        ).astype(jnp.bfloat16)

    shuffled = lax.map(one_block, (local_idx, block_rows))
    return shuffled.transpose(1, 2, 0, 3).reshape(copies * row_count, subj_rows)


def t_statistics(products, squares, crossed, freedom):
    count_maps = crossed.shape[0] // 4
    width = products.shape[1]
    gram = crossed[0:4]
    chol_z = jnp.linalg.cholesky(gram[1:4, 1:4])
    gamma_fit = jax.scipy.linalg.cho_solve((chol_z, True), products[1:4])
    resid_sq = squares[0] - jnp.sum(products[1:4] * gamma_fit, axis=0)
    cross_nuis = crossed.reshape(count_maps, 4, 4)[:, :, 1:4]
    projections = products.reshape(count_maps, 4, width) - jnp.einsum(
        "pkm,mn->pkn", cross_nuis, gamma_fit, precision=lax.Precision.HIGHEST
    )
    chol_full = jnp.linalg.cholesky(gram)
    inverse = jax.scipy.linalg.cho_solve((chol_full, True), jnp.eye(4, dtype=gram.dtype))
    slope_est = jnp.einsum("k,pkn->pn", inverse[0], projections, precision=lax.Precision.HIGHEST)
    mixed_proj = jnp.einsum("kl,pln->pkn", inverse, projections, precision=lax.Precision.HIGHEST)
    quadratic = jnp.sum(projections * mixed_proj, axis=1)
    return slope_est / jnp.sqrt((resid_sq - quadratic) / freedom * inverse[0, 0])


def body(subjects_data, covariates, permutes, brain_mask):
    subj_rows = subjects_data.shape[0]
    depth = subjects_data.shape[1]
    plane_cells = subjects_data.shape[2]
    voxels = depth * plane_cells
    count_maps = permutes.shape[0] + 1
    ones_row = jnp.ones((1, subj_rows), jnp.bfloat16)
    design = jnp.concatenate([covariates[0:1], ones_row, covariates[1:3]], axis=0)
    designs = jnp.concatenate([design, permute_design(permutes, design)], axis=0)
    flattened = subjects_data.reshape(subj_rows, voxels)
    products = jnp.dot(designs, flattened, preferred_element_type=jnp.float32)
    squares = jnp.sum(jnp.square(flattened.astype(jnp.float32)), axis=0)[None]
    crossed = jnp.dot(designs, design.T, preferred_element_type=jnp.float32)
    freedom = lax.axis_size("subj") * subj_rows - 4
    products, squares, crossed = lax.psum((products, squares, crossed), "subj")
    tmaps = t_statistics(products, squares, crossed, freedom)
    mask_float = brain_mask.astype(jnp.float32)
    masked = tmaps.reshape(count_maps, depth, plane_cells) * mask_float[None]
    padded = padded_2(masked, (("slab", 1),), 2)
    depth_smooth = gauss_taps[0] * padded[:, 0:depth]
    for position in range(1, 5):
        depth_smooth = depth_smooth + gauss_taps[position] * padded[:, position : position + depth]
    kernel = plane_kernel(PX, PY)
    smoothed = (
        jnp.dot(
            depth_smooth.reshape(-1, plane_cells), kernel, precision=lax.Precision.HIGHEST
        ).reshape(count_maps, depth, plane_cells)
        * mask_float[None]
    )
    smooth_t = smoothed[0]
    local_peaks = jnp.max(jnp.where(mask_float[None] > 0, smoothed[1:], -1e30), axis=(1, 2))
    perm_peaks = lax.pmax(local_peaks, "slab")
    p_values = (
        mask_float
        * (
            1.0
            + jnp.sum(jax.nn.sigmoid((perm_peaks[:, None, None] - smooth_t[None]) / 0.2), axis=0)
        )
        / count_maps
    )
    return (smooth_t, p_values, perm_peaks)


def solution(mesh):
    return jax.shard_map(
        body,
        mesh=mesh,
        in_specs=(P("subj", "slab", None), P(None, "subj"), P(None, "subj"), P("slab", None)),
        out_specs=(P("slab", None), P("slab", None), P()),
        check_vma=False,
    )
```

profile of v0, /device:TPU:0, one launch (start us, length us, event | category | flops | bytes accessed | tf_op | source)
XLA Modules:
  0.0 154.6 jit_solution(6308987013080061498)
XLA Ops:
  7.2 0.8 slice.75
  8.0 0.8 slice.76
  8.8 1.2 add_select_fusion
  10.0 0.2 copy.46
  10.2 0.1 pad_maximum_fusion.5
  10.3 38.7 %while.10 = (s32[]{:T(128)}, bf16[16,32,4,256]{3,2,1,0:T(4,128)(2,1)S(1)}, s32[16,32,256]{2,0,1:T(8,128)S(1)}, bf16[16,4,256]{2,1,0:T(4,128)(2,1)S(1)}, s32[]{:T(128)}) while((s32[]{:T(128)}, bf16[16,32,4,256]{3,2,1,0:T(4,128)(2,1)S(1)}, s32[16,32,256]{2,0,1:T(8,128)S(1)}, bf16[16,4,256]{2,1,0:T(4,128)(2,1)S(1)}, s32[]{:T(128)}) %tuple.32), condition=%wide.region_1.2_spmd, body=%wide.region_0.1_spmd.sunk | while | flops 18907136 | bytes 232513 | solution.py:67
  10.3 2.3 %fusion.110 = bf16[16,32,4,256]{3,2,1,0:T(4,128)(2,1)S(1)} fusion(bf16[16,32,4,256]{3,2,1,0:T(4,128)(2,1)S(1)} %get-tuple-element.79, s32[]{:T(128)} %get-tuple-element.78, s32[32,256]{1,0:T(8,128)S(1)} %bitcast.103, bf16[16,4,256]{2,1,0:T(4,128)(2,1)S(1)} %get-tuple-element.86), kind=kOutput, calls=%fused_computation.5.clone.1 | convolution fusion | flops 18907136 | bytes 101376 | tf_op jit(solution)/shard_map/while/body/eval_jaxpr/ci,pij->pcj/dot_general | solution.py:63
  12.8 2.3 %fusion.110 = bf16[16,32,4,256]{3,2,1,0:T(4,128)(2,1)S(1)} fusion(bf16[16,32,4,256]{3,2,1,0:T(4,128)(2,1)S(1)} %get-tuple-element.79, s32[]{:T(128)} %get-tuple-element.78, s32[32,256]{1,0:T(8,128)S(1)} %bitcast.103, bf16[16,4,256]{2,1,0:T(4,128)(2,1)S(1)} %get-tuple-element.86), kind=kOutput, calls=%fused_computation.5.clone.1 | convolution fusion | flops 18907136 | bytes 101376 | tf_op jit(solution)/shard_map/while/body/eval_jaxpr/ci,pij->pcj/dot_general | solution.py:63
  15.2 2.3 %fusion.110 = bf16[16,32,4,256]{3,2,1,0:T(4,128)(2,1)S(1)} fusion(bf16[16,32,4,256]{3,2,1,0:T(4,128)(2,1)S(1)} %get-tuple-element.79, s32[]{:T(128)} %get-tuple-element.78, s32[32,256]{1,0:T(8,128)S(1)} %bitcast.103, bf16[16,4,256]{2,1,0:T(4,128)(2,1)S(1)} %get-tuple-element.86), kind=kOutput, calls=%fused_computation.5.clone.1 | convolution fusion | flops 18907136 | bytes 101376 | tf_op jit(solution)/shard_map/while/body/eval_jaxpr/ci,pij->pcj/dot_general | solution.py:63
  17.6 2.3 %fusion.110 = bf16[16,32,4,256]{3,2,1,0:T(4,128)(2,1)S(1)} fusion(bf16[16,32,4,256]{3,2,1,0:T(4,128)(2,1)S(1)} %get-tuple-element.79, s32[]{:T(128)} %get-tuple-element.78, s32[32,256]{1,0:T(8,128)S(1)} %bitcast.103, bf16[16,4,256]{2,1,0:T(4,128)(2,1)S(1)} %get-tuple-element.86), kind=kOutput, calls=%fused_computation.5.clone.1 | convolution fusion | flops 18907136 | bytes 101376 | tf_op jit(solution)/shard_map/while/body/eval_jaxpr/ci,pij->pcj/dot_general | solution.py:63
  20.0 2.3 %fusion.110 = bf16[16,32,4,256]{3,2,1,0:T(4,128)(2,1)S(1)} fusion(bf16[16,32,4,256]{3,2,1,0:T(4,128)(2,1)S(1)} %get-tuple-element.79, s32[]{:T(128)} %get-tuple-element.78, s32[32,256]{1,0:T(8,128)S(1)} %bitcast.103, bf16[16,4,256]{2,1,0:T(4,128)(2,1)S(1)} %get-tuple-element.86), kind=kOutput, calls=%fused_computation.5.clone.1 | convolution fusion | flops 18907136 | bytes 101376 | tf_op jit(solution)/shard_map/while/body/eval_jaxpr/ci,pij->pcj/dot_general | solution.py:63
  22.4 2.3 %fusion.110 = bf16[16,32,4,256]{3,2,1,0:T(4,128)(2,1)S(1)} fusion(bf16[16,32,4,256]{3,2,1,0:T(4,128)(2,1)S(1)} %get-tuple-element.79, s32[]{:T(128)} %get-tuple-element.78, s32[32,256]{1,0:T(8,128)S(1)} %bitcast.103, bf16[16,4,256]{2,1,0:T(4,128)(2,1)S(1)} %get-tuple-element.86), kind=kOutput, calls=%fused_computation.5.clone.1 | convolution fusion | flops 18907136 | bytes 101376 | tf_op jit(solution)/shard_map/while/body/eval_jaxpr/ci,pij->pcj/dot_general | solution.py:63
  24.8 2.3 %fusion.110 = bf16[16,32,4,256]{3,2,1,0:T(4,128)(2,1)S(1)} fusion(bf16[16,32,4,256]{3,2,1,0:T(4,128)(2,1)S(1)} %get-tuple-element.79, s32[]{:T(128)} %get-tuple-element.78, s32[32,256]{1,0:T(8,128)S(1)} %bitcast.103, bf16[16,4,256]{2,1,0:T(4,128)(2,1)S(1)} %get-tuple-element.86), kind=kOutput, calls=%fused_computation.5.clone.1 | convolution fusion | flops 18907136 | bytes 101376 | tf_op jit(solution)/shard_map/while/body/eval_jaxpr/ci,pij->pcj/dot_general | solution.py:63
  27.3 2.3 %fusion.110 = bf16[16,32,4,256]{3,2,1,0:T(4,128)(2,1)S(1)} fusion(bf16[16,32,4,256]{3,2,1,0:T(4,128)(2,1)S(1)} %get-tuple-element.79, s32[]{:T(128)} %get-tuple-element.78, s32[32,256]{1,0:T(8,128)S(1)} %bitcast.103, bf16[16,4,256]{2,1,0:T(4,128)(2,1)S(1)} %get-tuple-element.86), kind=kOutput, calls=%fused_computation.5.clone.1 | convolution fusion | flops 18907136 | bytes 101376 | tf_op jit(solution)/shard_map/while/body/eval_jaxpr/ci,pij->pcj/dot_general | solution.py:63
  29.7 2.3 %fusion.110 = bf16[16,32,4,256]{3,2,1,0:T(4,128)(2,1)S(1)} fusion(bf16[16,32,4,256]{3,2,1,0:T(4,128)(2,1)S(1)} %get-tuple-element.79, s32[]{:T(128)} %get-tuple-element.78, s32[32,256]{1,0:T(8,128)S(1)} %bitcast.103, bf16[16,4,256]{2,1,0:T(4,128)(2,1)S(1)} %get-tuple-element.86), kind=kOutput, calls=%fused_computation.5.clone.1 | convolution fusion | flops 18907136 | bytes 101376 | tf_op jit(solution)/shard_map/while/body/eval_jaxpr/ci,pij->pcj/dot_general | solution.py:63
  32.1 2.3 %fusion.110 = bf16[16,32,4,256]{3,2,1,0:T(4,128)(2,1)S(1)} fusion(bf16[16,32,4,256]{3,2,1,0:T(4,128)(2,1)S(1)} %get-tuple-element.79, s32[]{:T(128)} %get-tuple-element.78, s32[32,256]{1,0:T(8,128)S(1)} %bitcast.103, bf16[16,4,256]{2,1,0:T(4,128)(2,1)S(1)} %get-tuple-element.86), kind=kOutput, calls=%fused_computation.5.clone.1 | convolution fusion | flops 18907136 | bytes 101376 | tf_op jit(solution)/shard_map/while/body/eval_jaxpr/ci,pij->pcj/dot_general | solution.py:63
  34.5 2.3 %fusion.110 = bf16[16,32,4,256]{3,2,1,0:T(4,128)(2,1)S(1)} fusion(bf16[16,32,4,256]{3,2,1,0:T(4,128)(2,1)S(1)} %get-tuple-element.79, s32[]{:T(128)} %get-tuple-element.78, s32[32,256]{1,0:T(8,128)S(1)} %bitcast.103, bf16[16,4,256]{2,1,0:T(4,128)(2,1)S(1)} %get-tuple-element.86), kind=kOutput, calls=%fused_computation.5.clone.1 | convolution fusion | flops 18907136 | bytes 101376 | tf_op jit(solution)/shard_map/while/body/eval_jaxpr/ci,pij->pcj/dot_general | solution.py:63
  36.9 2.3 %fusion.110 = bf16[16,32,4,256]{3,2,1,0:T(4,128)(2,1)S(1)} fusion(bf16[16,32,4,256]{3,2,1,0:T(4,128)(2,1)S(1)} %get-tuple-element.79, s32[]{:T(128)} %get-tuple-element.78, s32[32,256]{1,0:T(8,128)S(1)} %bitcast.103, bf16[16,4,256]{2,1,0:T(4,128)(2,1)S(1)} %get-tuple-element.86), kind=kOutput, calls=%fused_computation.5.clone.1 | convolution fusion | flops 18907136 | bytes 101376 | tf_op jit(solution)/shard_map/while/body/eval_jaxpr/ci,pij->pcj/dot_general | solution.py:63
  39.4 2.3 %fusion.110 = bf16[16,32,4,256]{3,2,1,0:T(4,128)(2,1)S(1)} fusion(bf16[16,32,4,256]{3,2,1,0:T(4,128)(2,1)S(1)} %get-tuple-element.79, s32[]{:T(128)} %get-tuple-element.78, s32[32,256]{1,0:T(8,128)S(1)} %bitcast.103, bf16[16,4,256]{2,1,0:T(4,128)(2,1)S(1)} %get-tuple-element.86), kind=kOutput, calls=%fused_computation.5.clone.1 | convolution fusion | flops 18907136 | bytes 101376 | tf_op jit(solution)/shard_map/while/body/eval_jaxpr/ci,pij->pcj/dot_general | solution.py:63
  41.8 2.3 %fusion.110 = bf16[16,32,4,256]{3,2,1,0:T(4,128)(2,1)S(1)} fusion(bf16[16,32,4,256]{3,2,1,0:T(4,128)(2,1)S(1)} %get-tuple-element.79, s32[]{:T(128)} %get-tuple-element.78, s32[32,256]{1,0:T(8,128)S(1)} %bitcast.103, bf16[16,4,256]{2,1,0:T(4,128)(2,1)S(1)} %get-tuple-element.86), kind=kOutput, calls=%fused_computation.5.clone.1 | convolution fusion | flops 18907136 | bytes 101376 | tf_op jit(solution)/shard_map/while/body/eval_jaxpr/ci,pij->pcj/dot_general | solution.py:63
  44.2 2.3 %fusion.110 = bf16[16,32,4,256]{3,2,1,0:T(4,128)(2,1)S(1)} fusion(bf16[16,32,4,256]{3,2,1,0:T(4,128)(2,1)S(1)} %get-tuple-element.79, s32[]{:T(128)} %get-tuple-element.78, s32[32,256]{1,0:T(8,128)S(1)} %bitcast.103, bf16[16,4,256]{2,1,0:T(4,128)(2,1)S(1)} %get-tuple-element.86), kind=kOutput, calls=%fused_computation.5.clone.1 | convolution fusion | flops 18907136 | bytes 101376 | tf_op jit(solution)/shard_map/while/body/eval_jaxpr/ci,pij->pcj/dot_general | solution.py:63
  46.6 2.3 %fusion.110 = bf16[16,32,4,256]{3,2,1,0:T(4,128)(2,1)S(1)} fusion(bf16[16,32,4,256]{3,2,1,0:T(4,128)(2,1)S(1)} %get-tuple-element.79, s32[]{:T(128)} %get-tuple-element.78, s32[32,256]{1,0:T(8,128)S(1)} %bitcast.103, bf16[16,4,256]{2,1,0:T(4,128)(2,1)S(1)} %get-tuple-element.86), kind=kOutput, calls=%fused_computation.5.clone.1 | convolution fusion | flops 18907136 | bytes 101376 | tf_op jit(solution)/shard_map/while/body/eval_jaxpr/ci,pij->pcj/dot_general | solution.py:63
  49.0 0.9 copy.31
  49.8 0.4 copy.47
  50.3 9.3 %copy.48 = bf16[512,8,2,512]{3,1,2,0:T(8,128)(2,1)} copy(bf16[512,8,2,512]{3,2,1,0:T(2,128)(2,1)} %bitcast.95) | data formatting | bytes 16777216
  59.6 5.6 %fusion.47 = f32[132,1024]{1,0:T(8,128)} fusion(bf16[4096,1024]{1,0:T(8,128)(2,1)} %bitcast.96, bf16[128,4096]{1,0:T(8,128)(2,1)S(1)} %bitcast.99, bf16[2,4096]{1,0:T(2,128)(2,1)S(1)} %slice.76, bf16[1,4096]{1,0:T(2,128)(2,1)S(1)} %broadcast_in_dim.20, bf16[1,4096]{1,0:T(2,128)(2,1)S(1)} %slice.75), kind=kOutput, calls=%fused_computation.68 | convolution fusion | flops 1111621632 | bytes 10010624 | tf_op jit(solution)/shard_map/dot_general | solution.py:100
  65.2 0.5 fusion.48
  65.7 18.5 %multiply_reduce_fusion = f32[2,512]{1,0:T(2,128)S(1)} fusion(bf16[4096,2,512]{2,1,0:T(2,128)(2,1)} %param.6), kind=kLoop, calls=%fused_computation.11 | loop fusion | flops 12581888 | bytes 8392704 | tf_op jit(solution)/shard_map/reduce_sum | solution.py:101
  84.2 11.7 %all-reduce = (f32[132,4]{0,1:T(4,128)S(1)}, f32[1,1024]{1,0:T(1,128)S(1)}) all-reduce(f32[132,4]{0,1:T(4,128)S(1)} %fusion.48, f32[1,1024]{1,0:T(1,128)S(1)} %bitcast.108), channel_id=1, replica_groups=mesh['subj'=4,'slab'=8] {'subj'}, use_global_device_ids=true, to_apply=%region_2.3 | all-reduce | flops 1552 | bytes 12416 | tf_op jit(solution)/shard_map/psum | solution.py:104
  95.9 0.1 slice.88
  95.9 0.1 copy.36
  96.0 0.1 fusion.85
  96.1 0.3 cholesky.63
  96.4 0.6 compare_reduce_fusion
  97.1 0.6 fusion.75
  97.7 0.1 copy.32
  97.8 0.1 copy.33
  97.9 0.4 cholesky.30
  98.3 0.6 compare_reduce_fusion.1
  99.0 0.6 fusion.74
  99.6 0.1 reshape.116
  99.7 0.3 custom-call.21
  100.0 0.3 custom-call.20
  100.3 0.1 copy.45
  100.5 0.2 fusion.80
  100.6 0.1 fusion.82
  100.8 0.5 slice.81
  102.0 11.9 %all-reduce.3.cloned.1.call-done = f32[132,1024]{1,0:T(8,128)} async-done(((f32[132,1024]{1,0:T(8,128)}), f32[132,1024]{1,0:T(8,128)}) %all-reduce.3.cloned.1.call-update) | async-done | bytes 540688 | tf_op jit(solution)/shard_map/psum | solution.py:104
  113.9 1.2 reshape.115
  115.1 1.0 fusion.68
  116.1 0.9 multiply_reduce_fusion.1
  117.0 1.0 convolution_subtract_fusion
  118.0 1.3 fusion.45
  119.3 1.3 fusion.43
  120.6 0.3 fusion.28
  121.0 0.1 reshape.117
  121.2 1.6 %collective-permute-start = (f32[33,2,512]{2,0,1:T(8,128)S(1)}, f32[33,2,512]{2,0,1:T(8,128)S(1)}, u32[]{:S(2)}, u32[]{:S(2)}) collective-permute-start(f32[33,2,512]{2,0,1:T(8,128)S(1)} %copy_multiply_fusion), channel_id=1, source_target_pairs={{0,1},{1,2},{2,3},{3,4},{4,5},{5,6},{6,7},{8,9},{9,10},{10,11},{11... | collective-permute-start | bytes 405512 | tf_op jit(solution)/shard_map/ppermute | solution.py:25
  122.7 1.3 collective-permute-start.1
  124.1 3.4 %collective-permute-done.1 = f32[33,2,512]{2,0,1:T(8,128)S(1)} collective-permute-done((f32[33,2,512]{2,0,1:T(8,128)S(1)}, f32[33,2,512]{2,0,1:T(8,128)S(1)}, u32[]{:S(2)}, u32[]{:S(2)}) %collective-permute-start.1) | collective-permute-done | bytes 135200 | tf_op jit(solution)/shard_map/ppermute | solution.py:27
  127.5 1.9 %convolution_multiply_fusion = f32[33,2,512]{2,0,1:T(8,128)S(1)} fusion(s32[512]{0:T(512)S(1)} %get-tuple-element.46, s32[512]{0:T(512)S(1)} %get-tuple-element.47, f32[33,2,512]{2,0,1:T(8,128)S(1)} %collective-permute-done.1, f32[33,2,512]{2,0,1:T(8,128)S(1)} %copy_multiply_fusion, f32[33,2,512]{2,0,1:T(8,128)S(1)} %collective-permute-done, ...), kind=kOutput, calls=%fused_computation.23 | convolution fusion | flops 216150016 | bytes 548864 | tf_op jit(solution)/shard_map/dot_general | solution.py:114
  129.4 0.1 fusion.62
  129.6 17.4 %pmax.7 = f32[32]{0:T(128)S(1)} all-reduce(f32[32]{0:T(128)S(1)} %fusion.62), channel_id=1, replica_groups=mesh['subj'=4,'slab'=8] {'slab'}, use_global_device_ids=true, to_apply=%region_13.14 | all-reduce | flops 32 | bytes 256 | tf_op jit(solution)/shard_map/pmax | solution.py:121
  147.0 0.1 fusion.63
  147.1 0.6 multiply_multiply_fusion
  (57 shorter events, 0.9 us)
Async XLA Ops:
  7.2 106.7 %all-reduce.3.cloned.1.call-start = ((), (), s32[]{:S(2)}) async-start(), calls=%async_computation | async-start | bytes 1114112 | tf_op jit(solution)/shard_map/psum | solution.py:104
  65.7 35.6 %copy-start = (s32[2,512]{1,0:T(2,128)S(1)}, s32[2,512]{1,0:T(2,128)}, u32[]{:S(2)}) copy-start(s32[2,512]{1,0:T(2,128)} %param.9) | copy-start | bytes 12292
  121.2 2.9 %collective-permute-start = (f32[33,2,512]{2,0,1:T(8,128)S(1)}, f32[33,2,512]{2,0,1:T(8,128)S(1)}, u32[]{:S(2)}, u32[]{:S(2)}) collective-permute-start(f32[33,2,512]{2,0,1:T(8,128)S(1)} %copy_multiply_fusion), channel_id=1, source_target_pairs={{0,1},{1,2},{2,3},{3,4},{4,5},{5,6},{6,7},{8,9},{9,10},{10,11},{11... | collective-permute-start | bytes 405512 | tf_op jit(solution)/shard_map/ppermute | solution.py:25
  122.7 4.7 %collective-permute-start.1 = (f32[33,2,512]{2,0,1:T(8,128)S(1)}, f32[33,2,512]{2,0,1:T(8,128)S(1)}, u32[]{:S(2)}, u32[]{:S(2)}) collective-permute-start(f32[33,2,512]{2,0,1:T(8,128)S(1)} %copy_multiply_fusion), channel_id=1, source_target_pairs={{1,0},{2,1},{3,2},{4,3},{5,4},{6,5},{7,6},{9,8},{10,9},{11,10},{12... | collective-permute-start | bytes 405512 | tf_op jit(solution)/shard_map/ppermute | solution.py:27
  129.4 18.3 %copy-start.1 = (f32[1,2,512]{2,1,0:T(2,128)}, f32[1,2,512]{2,1,0:T(2,128)S(1)}, u32[]{:S(2)}) copy-start(f32[1,2,512]{2,1,0:T(2,128)S(1)} %copy.61) | copy-start | bytes 12292
  147.0 0.7 copy-start.2
Sparse Core Ops, SparseCore 0:
  65.3 48.5 all-reduce.2
where the time goes:
time: 155 us
  matrix products  51.3 us (33%)
  blocking collectives  29.1 us (19%)
  other arithmetic  25 us (16%)
  local copies, waits for them, and re-layouts  15.4 us (10%)
  waiting for transfers between devices  15.3 us (10%)
  between operations  14.9 us (10%)
  starting transfers between devices  2.89 us (2%)
    dot_general x16, matrix products, one_block(): jnp.einsum('ci,pij->pcj', design_part, onehot, preferred_element_type=jnp...  37.5 us
    reduce_sum x1, other arithmetic, body(): squares = jnp.sum(jnp.square(flattened.astype(jnp.float32)), axis=0)[None]  18.5 us
    pmax x1, blocking collectives, body(): perm_peaks = lax.pmax(local_peaks, 'slab')  17.4 us
    psum x1, waiting for transfers between devices, body(): products, squares, crossed = lax.psum((products, squares, crossed), 'subj')  11.9 us
    psum x1, blocking collectives, body(): products, squares, crossed = lax.psum((products, squares, crossed), 'subj')  11.7 us
    unnamed x12, local copies, waits for them, and re-layouts  10 us
    dot_general x1, matrix products, body(): products = jnp.dot(designs, flattened, preferred_element_type=jnp.float32)  5.58 us
    ppermute x1, waiting for transfers between devices, padded_2(): lax.ppermute(head, axis, [((i + 1) % count, i) for i in range(ends)])  3.4 us
  transfers between devices with their start and end apart: 3, of which 2 were waited for; matrix products, arithmetic and copies ran while one was open for 16% of the time, Pallas kernels for 0%

commit v1 on v0

v1 whole, which is shorter than its diff:
```python
import functools
import math

import jax
import jax.numpy as jnp
from jax import lax
from jax.experimental import pallas as pl
from jax.experimental.pallas import tpu as pltpu
from jax.sharding import PartitionSpec as P

BLOCK = 256
HALF = 128
PX = 16
PY = 32
LANES = 128
MESH = pl.DeviceIdType.MESH

gauss_raw = tuple((math.exp(-0.5 * (offset - 2) ** 2) for offset in range(5)))
gauss_taps = tuple((value / sum(gauss_raw) for value in gauss_raw))

NT = (((1,), (1,)), ((), ()))


def products_kernel(groups, per, rows, x_ref, cov_ref, perm_ref, chunk_ref, obs_ref, flat, shuf_a, shuf_b, des):
    step = pl.program_id(0)
    copies = perm_ref.shape[0]
    top = groups * rows
    voxels = chunk_ref.shape[2] - LANES
    half_tiles = voxels // (2 * LANES)

    @pl.when(step == 0)
    def _():
        chunk_ref[...] = jnp.zeros_like(chunk_ref)
        obs_ref[...] = jnp.zeros_like(obs_ref)
        shuf_a[...] = jnp.zeros_like(shuf_a)
        shuf_b[...] = jnp.zeros_like(shuf_b)
        des[...] = jnp.zeros_like(des)

    cov = cov_ref[...].astype(jnp.float32)
    des[0:3, :] = cov
    des[4:7, :] = cov
    des[8:9, :] = cov[0:1]
    des[9:10, :] = jnp.ones((1, BLOCK), jnp.float32)
    des[10:12, :] = cov[1:3]
    shuf_a[top : top + 4, :] = des[8:12, 0:HALF]
    shuf_b[top : top + 4, :] = des[8:12, HALF:BLOCK]

    local = perm_ref[...] & (BLOCK - 1)
    high = local // HALF
    low = (local & (HALF - 1)).astype(jnp.float32)
    row_high = lax.broadcasted_iota(jnp.int32, (8, BLOCK), 0) // 4
    place = (
        lax.broadcasted_iota(jnp.int32, (HALF // 16, 16, BLOCK), 0) * 16
        + lax.broadcasted_iota(jnp.int32, (HALF // 16, 16, BLOCK), 1)
    ).astype(jnp.float32).astype(jnp.bfloat16)
    one = jnp.ones((), jnp.bfloat16)
    zero = jnp.zeros((), jnp.bfloat16)
    base = des[0:8, :]
    for pair in range(copies // 2):
        lefts = []
        hots = []
        for p in (2 * pair, 2 * pair + 1):
            lefts.append(jnp.where(high[p : p + 1] == row_high, base, 0.0))
            spread = jnp.broadcast_to(low[p : p + 1], (16, BLOCK)).astype(jnp.bfloat16)
            hots.append(jnp.where(spread[None] == place, one, zero).reshape(HALF, BLOCK))
        left = jnp.concatenate(lefts, axis=0).astype(jnp.bfloat16)
        hot = jnp.concatenate(hots, axis=0)
        moved = lax.dot_general(left, hot, NT, preferred_element_type=jnp.float32)
        for side in range(2):
            p = 2 * pair + side
            row = p // per * rows + p % per
            part = moved[8 * side : 8 * side + 8, HALF * side : HALF * side + HALF]
            shuf_a[pl.ds(row, 3, stride=per), :] = part[0:3]
            shuf_b[pl.ds(row, 3, stride=per), :] = part[4:7]

    flat[...] = x_ref[...].astype(jnp.float32)
    designs = jnp.concatenate([shuf_a[...], shuf_b[...]], axis=1).astype(jnp.bfloat16)
    for tile in range(half_tiles):
        z = tile // (half_tiles // 2)
        cells = [2 * (tile % (half_tiles // 2)) + i for i in range(2)]
        part = jnp.concatenate(
            [flat[pl.ds(2 * c + z, BLOCK, stride=8), :] for c in cells], axis=1
        )
        cols = slice(2 * LANES * tile, 2 * LANES * (tile + 1))
        res = jnp.dot(designs, part.astype(jnp.bfloat16), preferred_element_type=jnp.float32)
        for g in range(groups):
            chunk_ref[g, :, cols] += res[g * rows : (g + 1) * rows]
        squares = jnp.sum(part * part, axis=0, keepdims=True)
        sub = lax.broadcasted_iota(jnp.int32, (8, 2 * LANES), 0)
        obs_ref[:, cols] += res[top : top + 8] + jnp.where(sub == 4, squares, 0.0)
    right = jnp.concatenate(
        [des[8:16, :], jnp.zeros((LANES - 8, BLOCK), jnp.float32)], axis=0
    ).astype(jnp.bfloat16)
    res = lax.dot_general(designs, right, NT, preferred_element_type=jnp.float32)
    for g in range(groups):
        chunk_ref[g, :, voxels:] += res[g * rows : (g + 1) * rows]
    obs_ref[:, voxels:] += res[top : top + 8]


def cholesky(mat):
    size = len(mat)
    low = [[None] * size for _ in range(size)]
    for j in range(size):
        total = mat[j][j]
        for k in range(j):
            total = total - low[j][k] * low[j][k]
        low[j][j] = jnp.sqrt(total)
        for i in range(j + 1, size):
            total = mat[i][j]
            for k in range(j):
                total = total - low[i][k] * low[j][k]
            low[i][j] = total / low[j][j]
    return low


def cho_solve(low, inv_diag, rhs):
    size = len(low)
    half = []
    for i in range(size):
        total = rhs[i]
        for k in range(i):
            total = total - low[i][k] * half[k]
        half.append(total * inv_diag[i])
    out = [None] * size
    for i in reversed(range(size)):
        total = half[i]
        for k in range(i + 1, size):
            total = total - low[k][i] * out[k]
        out[i] = total * inv_diag[i]
    return out


def blur(cells, stride, coord, size):
    width = cells.shape[1]
    total = None
    for position in range(5):
        d = position - 2
        moved = cells if d == 0 else pltpu.roll(cells, (-d * stride) % width, 1)
        inside = (coord + d >= 0) & (coord + d < size)
        term = gauss_taps[position] * jnp.where(inside, moved, 0.0)
        total = term if total is None else total + term
    return total


def maps_kernel(
    n, m, per, copies, freedom,
    chunk_ref, obs_ref, mask_ref, smooth_ref, pval_ref, peak_ref,
    got, gobs, own, own_o, low, low_o, high, high_o, field, pk1, pk2,
    send, recv, send_o, recv_o, hsend, hrecv, psend, prec, qsend, qrec,
):
    me = lax.axis_index("subj")
    slab = lax.axis_index("slab")
    plane = mask_ref.shape[1]
    voxels = 2 * plane

    barrier = pltpu.get_barrier_semaphore()
    for o in range(1, n):
        pl.semaphore_signal(barrier, inc=1, device_id=(lax.rem(me + o, n), slab), device_id_type=MESH)
    for o in range(1, m):
        pl.semaphore_signal(barrier, inc=1, device_id=(me, lax.rem(slab + o, m)), device_id_type=MESH)
    pl.semaphore_wait(barrier, n + m - 2)

    copies_a = []
    for o in range(1, n):
        to = lax.rem(me + o, n)
        copies_a.append(pltpu.make_async_remote_copy(
            src_ref=obs_ref, dst_ref=gobs.at[o], send_sem=send_o.at[o], recv_sem=recv_o.at[o],
            device_id=(to, slab), device_id_type=MESH))
        copies_a[-1].start()
    copies_b = []
    for o in range(1, n):
        to = lax.rem(me + o, n)
        copies_b.append(pltpu.make_async_remote_copy(
            src_ref=chunk_ref.at[to], dst_ref=got.at[o], send_sem=send.at[o], recv_sem=recv.at[o],
            device_id=(to, slab), device_id_type=MESH))
        copies_b[-1].start()
    got[0] = chunk_ref[me]
    gobs[0] = obs_ref[...]

    cells = mask_ref[...].astype(jnp.float32)
    mask_row = jnp.concatenate([cells[0:1], cells[1:2]], axis=1)

    for copy in copies_a:
        copy.wait()
    obs = gobs[lax.rem(me + n, n)]
    for s in range(1, n):
        obs = obs + gobs[lax.rem(me - s + n, n)]
    prod = [obs[k : k + 1, :voxels] for k in range(4)]
    gram = [[obs[i : i + 1, voxels + j : voxels + j + 1] for j in range(4)] for i in range(4)]
    low_z = cholesky([row[1:4] for row in gram[1:4]])
    fit = cho_solve(low_z, [1.0 / low_z[i][i] for i in range(3)], prod[1:4])
    resid = obs[4:5, :voxels] - (prod[1] * fit[0] + prod[2] * fit[1] + prod[3] * fit[2])
    low_f = cholesky(gram)
    inv_diag = [1.0 / low_f[i][i] for i in range(4)]
    unit = [jnp.zeros((1, 1), jnp.float32), jnp.ones((1, 1), jnp.float32)]
    columns = [cho_solve(low_f, inv_diag, [unit[int(i == j)] for i in range(4)]) for j in range(4)]
    inverse = [[columns[j][i] for j in range(4)] for i in range(4)]

    def statistic(proj):
        slope = sum(inverse[0][k] * proj[k] for k in range(4))
        quad = sum(proj[k] * sum(inverse[k][l] * proj[l] for l in range(4)) for k in range(4))
        return slope / jnp.sqrt((resid - quad) / freedom * inverse[0][0])

    seen = [
        prod[k] - sum(gram[k][1 + i] * fit[i] for i in range(3)) for k in range(4)
    ]
    own_o[...] = statistic(seen) * mask_row

    for copy in copies_b:
        copy.wait()
    chunk = got[0]
    for o in range(1, n):
        chunk = chunk + got[o]
    proj = []
    for c in range(3):
        rows = chunk[c * per : (c + 1) * per]
        proj.append(
            rows[:, :voxels]
            - sum(rows[:, voxels + 1 + i : voxels + 2 + i] * fit[i] for i in range(3))
        )
    own[...] = statistic([proj[0], seen[1], proj[1], proj[2]]) * mask_row

    up = (me, lax.rem(slab + 1, m))
    down = (me, lax.rem(slab + m - 1, m))

    def halo(src, dst, k, to):
        return pltpu.make_async_remote_copy(
            src_ref=src, dst_ref=dst, send_sem=hsend.at[k], recv_sem=hrecv.at[k],
            device_id=to, device_id_type=MESH)

    rise = [halo(own, low, 0, up), halo(own_o, low_o, 1, up)]
    fall = [halo(own, high, 2, down), halo(own_o, high_o, 3, down)]

    @pl.when(slab < m - 1)
    def _():
        for copy in rise:
            copy.start()

    @pl.when(slab > 0)
    def _():
        for copy in fall:
            copy.start()

    @pl.when(slab == 0)
    def _():
        low[...] = jnp.zeros_like(low)
        low_o[...] = jnp.zeros_like(low_o)

    @pl.when(slab == m - 1)
    def _():
        high[...] = jnp.zeros_like(high)
        high_o[...] = jnp.zeros_like(high_o)

    field[...] = jnp.zeros_like(field)

    @pl.when(slab > 0)
    def _():
        for copy in rise:
            copy.wait_recv()

    @pl.when(slab < m - 1)
    def _():
        for copy in fall:
            copy.wait_recv()

    def deep(lower, mine, upper):
        slices = []
        for ref in (lower, mine, upper):
            value = ref[...]
            slices += [value[:, :plane], value[:, plane:]]
        return [
            sum(gauss_taps[position] * slices[position + z] for position in range(5))
            for z in range(2)
        ]

    first, second = deep(low, own, high)
    field[0:per, :] = first
    field[8 : 8 + per, :] = second
    first, second = deep(low_o, own_o, high_o)
    field[16:17, :] = first
    field[17:18, :] = second

    cell = lax.broadcasted_iota(jnp.int32, (24, plane), 1)
    smooth = blur(field[...], PY, cell // PY, PX)
    smooth = blur(smooth, 1, cell % PY, PY)

    peaks = jnp.maximum(
        jnp.max(jnp.where(cells[0:1] > 0, smooth[0:per] * cells[0:1], -1e30), axis=1, keepdims=True),
        jnp.max(jnp.where(cells[1:2] > 0, smooth[8 : 8 + per] * cells[1:2], -1e30), axis=1, keepdims=True),
    )
    pk1[0] = jnp.broadcast_to(peaks, (per, LANES))
    copies_p = []
    for o in range(1, m):
        copies_p.append(pltpu.make_async_remote_copy(
            src_ref=pk1.at[0], dst_ref=pk1.at[o], send_sem=psend.at[o], recv_sem=prec.at[o],
            device_id=(me, lax.rem(slab + o, m)), device_id_type=MESH))
        copies_p[-1].start()
    seen_t = [smooth[16 + z : 17 + z] * cells[z : z + 1] for z in range(2)]
    smooth_ref[...] = jnp.concatenate(seen_t, axis=0)
    seen_row = jnp.concatenate(seen_t, axis=1)

    for copy in copies_p:
        copy.wait_recv()
    best = pk1[0]
    for o in range(1, m):
        best = jnp.maximum(best, pk1[o])
    pk2[0] = best
    copies_q = []
    for o in range(1, n):
        copies_q.append(pltpu.make_async_remote_copy(
            src_ref=pk2.at[0], dst_ref=pk2.at[o], send_sem=qsend.at[o], recv_sem=qrec.at[o],
            device_id=(lax.rem(me + o, n), slab), device_id_type=MESH))
        copies_q[-1].start()
    for copy in copies_q:
        copy.wait_recv()

    count = jnp.zeros((1, voxels), jnp.float32)
    line = jnp.zeros((1, LANES), jnp.float32)
    sub = lax.broadcasted_iota(jnp.int32, (per, LANES), 0)
    lane = lax.broadcasted_iota(jnp.int32, (per, LANES), 1)
    for d in range(n):
        value = pk2[lax.rem(me - d + n, n)]
        level = jax.nn.sigmoid((value[:, 0:1] - seen_row) / 0.2)
        count = count + jnp.sum(level, axis=0, keepdims=True)
        line = line + jnp.sum(jnp.where(lane == sub + d * per, value, 0.0), axis=0, keepdims=True)
    pval = mask_row * (1.0 + count) / (copies + 1)
    pval_ref[...] = jnp.concatenate([pval[:, :plane], pval[:, plane:]], axis=0)
    peak_ref[...] = line[:, :copies]

    for copy in copies_p + copies_q:
        copy.wait_send()

    @pl.when(slab < m - 1)
    def _():
        for copy in rise:
            copy.wait_send()

    @pl.when(slab > 0)
    def _():
        for copy in fall:
            copy.wait_send()


def body(n, m, subjects_data, covariates, permutes, brain_mask):
    subj_rows, depth, plane = subjects_data.shape
    assert depth == 2 and plane == PX * PY
    copies = permutes.shape[0]
    per = copies // n
    rows = -(-3 * per // 8) * 8
    voxels = depth * plane
    width = voxels + LANES
    tiles = plane // LANES
    flat_rows = depth * tiles
    data = (
        subjects_data.reshape(subj_rows, depth, tiles, LANES)
        .transpose(0, 2, 1, 3)
        .reshape(subj_rows * flat_rows, LANES)
    )
    height = -(-(n * rows + 8) // 16) * 16
    f32 = jnp.float32
    chunk, obs = pl.pallas_call(
        functools.partial(products_kernel, n, per, rows),
        grid=(subj_rows // BLOCK,),
        in_specs=[
            pl.BlockSpec((BLOCK * flat_rows, LANES), lambda b: (b, 0)),
            pl.BlockSpec((3, BLOCK), lambda b: (0, b)),
            pl.BlockSpec((copies, BLOCK), lambda b: (0, b)),
        ],
        out_specs=[
            pl.BlockSpec((n, rows, width), lambda b: (0, 0, 0)),
            pl.BlockSpec((8, width), lambda b: (0, 0)),
        ],
        out_shape=[
            jax.ShapeDtypeStruct((n, rows, width), f32),
            jax.ShapeDtypeStruct((8, width), f32),
        ],
        scratch_shapes=[
            pltpu.VMEM((BLOCK * flat_rows, LANES), f32),
            pltpu.VMEM((height, HALF), f32),
            pltpu.VMEM((height, HALF), f32),
            pltpu.VMEM((16, BLOCK), f32),
        ],
        compiler_params=pltpu.CompilerParams(vmem_limit_bytes=60 * 2**20),
        name="products",
    )(data, covariates, permutes)

    vmem = pl.BlockSpec(memory_space=pltpu.VMEM)
    dma = pltpu.SemaphoreType.DMA
    smooth_t, p_values, peaks = pl.pallas_call(
        functools.partial(maps_kernel, n, m, per, copies, float(n * subj_rows - 4)),
        in_specs=[vmem] * 3,
        out_specs=[vmem] * 3,
        out_shape=[
            jax.ShapeDtypeStruct((depth, plane), f32),
            jax.ShapeDtypeStruct((depth, plane), f32),
            jax.ShapeDtypeStruct((1, copies), f32),
        ],
        scratch_shapes=[
            pltpu.VMEM((n, rows, width), f32),
            pltpu.VMEM((n, 8, width), f32),
            pltpu.VMEM((per, voxels), f32),
            pltpu.VMEM((1, voxels), f32),
            pltpu.VMEM((per, voxels), f32),
            pltpu.VMEM((1, voxels), f32),
            pltpu.VMEM((per, voxels), f32),
            pltpu.VMEM((1, voxels), f32),
            pltpu.VMEM((24, plane), f32),
            pltpu.VMEM((m, per, LANES), f32),
            pltpu.VMEM((n, per, LANES), f32),
            dma((n,)), dma((n,)), dma((n,)), dma((n,)),
            dma((4,)), dma((4,)), dma((m,)), dma((m,)), dma((n,)), dma((n,)),
        ],
        compiler_params=pltpu.CompilerParams(
            collective_id=0, has_side_effects=True, vmem_limit_bytes=32 * 2**20
        ),
        name="maps",
    )(chunk, obs, brain_mask)
    return smooth_t, p_values, peaks.reshape(copies)


def solution(mesh):
    return jax.shard_map(
        functools.partial(body, mesh.shape["subj"], mesh.shape["slab"]),
        mesh=mesh,
        in_specs=(P("subj", "slab", None), P(None, "subj"), P(None, "subj"), P("slab", None)),
        out_specs=(P("slab", None), P("slab", None), P()),
        check_vma=False,
    )
```

time: 155 us -> 45.4 us (0.29)
  matrix products: 51.3 us -> 0 us
  Pallas kernels: 0 us -> 40.8 us
  blocking collectives: 29.1 us -> 0 us
  other arithmetic: 25 us -> 0 us
  waiting for transfers between devices: 15.3 us -> 0 us
  between operations: 14.9 us -> 0.65 us
  local copies, waits for them, and re-layouts: 15.4 us -> 3.48 us
  starting transfers between devices: 2.89 us -> 0 us
    dot_general x22 -> x0, matrix products: 49.1 us -> none  [the longest x16 37.5 us: one_block(): jnp.einsum('ci,pij->pcj', design_part, onehot, preferred_element_type=jnp...]
    pallas_call x0 -> x2, Pallas kernels: none -> 40.8 us  [the longest x1 23 us: body(): pl.pallas_call(functools.partial(maps_kernel, n, m, per, copies, float(n...]
    reduce_sum x3 -> x0, other arithmetic: 18.9 us -> none  [the longest x1 18.5 us: body(): squares = jnp.sum(jnp.square(flattened.astype(jnp.float32)), axis=0)[None]]
    pmax x1 -> x0, blocking collectives: 17.4 us -> none  [body(): perm_peaks = lax.pmax(local_peaks, 'slab')]
    psum x1 -> x0, waiting for transfers between devices: 11.9 us -> none  [body(): products, squares, crossed = lax.psum((products, squares, crossed), 'subj')]
    psum x1 -> x0, blocking collectives: 11.7 us -> none  [body(): products, squares, crossed = lax.psum((products, squares, crossed), 'subj')]
    unnamed x12 -> x9, local copies, waits for them, and re-layouts: 10 us -> 3.48 us
    another operation x10 -> x0, other arithmetic: 3.88 us -> none  [the longest x3 1.03 us: t_statistics(): chol_full = jnp.linalg.cholesky(gram)]
  transfers between devices with their start and end apart: 3 -> 0, of which waited for: 2 -> 0; matrix products, arithmetic and copies ran while one was open for 16% -> 0% of each run, Pallas kernels for 0% -> 0%
where the time goes in v1:
time: 45.4 us; the launch traced here: 44.9 us
  Pallas kernels  40.8 us (90%)
  local copies, waits for them, and re-layouts  3.48 us (8%)
  between operations  0.65 us (1%)
    pallas_call x1, Pallas kernels, body(): pl.pallas_call(functools.partial(maps_kernel, n, m, per, copies, float(n...  23 us
    pallas_call x1, Pallas kernels, body(): pl.pallas_call(functools.partial(products_kernel, n, per, rows), grid=(su...  17.8 us
    unnamed x9, local copies, waits for them, and re-layouts  3.48 us

profile of v1, /device:TPU:0, one launch (start us, length us, event | category | flops | bytes accessed | tf_op | source)
XLA Modules:
  0.0 44.9 jit_solution(17367991037949634603)
XLA Ops:
  0.6 0.0 copy-start.2
  0.6 17.8 %products.1 = (f32[4,24,1152]{2,1,0:T(8,128)}, f32[8,1152]{1,0:T(8,128)}) custom-call(bf16[32768,128]{1,0:T(8,128)(2,1)} %bitcast.7, bf16[3,4096]{1,0:T(4,128)(2,1)} %cov_ref.1, s32[32,4096]{1,0:T(8,128)} %perm_ref.1), custom_call_target="tpu_custom_call" | custom-call | tf_op jit(solution)/shard_map/products/pallas_call | solution.py:361
  18.4 0.0 copy-done.2
  18.4 0.0 copy-start
  18.4 1.0 %copy-done = f32[4,24,1152]{2,1,0:T(8,128)S(1)} copy-done((f32[4,24,1152]{2,1,0:T(8,128)S(1)}, f32[4,24,1152]{2,1,0:T(8,128)}, u32[]{:S(2)}) %copy-start) | copy-done | bytes 442392
  19.5 0.0 copy-start.1
  19.5 0.8 %copy-done.1 = f32[8,1152]{1,0:T(8,128)S(1)} copy-done((f32[8,1152]{1,0:T(8,128)S(1)}, f32[8,1152]{1,0:T(8,128)}, u32[]{:S(2)}) %copy-start.1) | copy-done | bytes 36888
  20.2 23.0 %maps.1 = (f32[2,512]{1,0:T(2,128)S(1)}, f32[2,512]{1,0:T(2,128)S(1)}, f32[1,32]{1,0:T(1,128)S(1)}) custom-call(f32[4,24,1152]{2,1,0:T(8,128)S(1)} %copy-done, f32[8,1152]{1,0:T(8,128)S(1)} %copy-done.1, s32[2,512]{1,0:T(2,128)S(1)} %copy-done.2), custom_call_target="tpu_custom_call" | custom-call | tf_op jit(solution)/shard_map/maps/pallas_call | solution.py:389
  43.2 0.6 %copy.11 = f32[2,512]{1,0:T(2,128)} copy(f32[2,512]{1,0:T(2,128)S(1)} %get-tuple-element.16) | data formatting | bytes 8192
  43.8 0.6 %copy.12 = f32[2,512]{1,0:T(2,128)} copy(f32[2,512]{1,0:T(2,128)S(1)} %get-tuple-element.17) | data formatting | bytes 8192
  44.4 0.5 %copy.13 = f32[32]{0:T(128)} copy(f32[32]{0:T(128)S(1)} %bitcast.6) | data formatting | bytes 256
Async XLA Ops:
  0.6 17.8 %copy-start.2 = (s32[2,512]{1,0:T(2,128)S(1)}, s32[2,512]{1,0:T(2,128)}, u32[]{:S(2)}) copy-start(s32[2,512]{1,0:T(2,128)} %mask_ref.1) | copy-start | bytes 12292
  18.4 1.0 %copy-start = (f32[4,24,1152]{2,1,0:T(8,128)S(1)}, f32[4,24,1152]{2,1,0:T(8,128)}, u32[]{:S(2)}) copy-start(f32[4,24,1152]{2,1,0:T(8,128)} %get-tuple-element.8.chunk_ref) | copy-start | bytes 1327108
  19.5 0.8 %copy-start.1 = (f32[8,1152]{1,0:T(8,128)S(1)}, f32[8,1152]{1,0:T(8,128)}, u32[]{:S(2)}) copy-start(f32[8,1152]{1,0:T(8,128)} %get-tuple-element.9.obs_ref) | copy-start | bytes 110596

commit v2 on v1

v2 whole, which is shorter than its diff:
```python
import functools
import math

import jax
import jax.numpy as jnp
from jax import lax
from jax.experimental import pallas as pl
from jax.experimental.pallas import tpu as pltpu
from jax.sharding import PartitionSpec as P

BLOCK = 256
HALF = 128
PX = 16
PY = 32
LANES = 128
MESH = pl.DeviceIdType.MESH

gauss_raw = tuple((math.exp(-0.5 * (offset - 2) ** 2) for offset in range(5)))
gauss_taps = tuple((value / sum(gauss_raw) for value in gauss_raw))

NT = (((1,), (1,)), ((), ()))


def cholesky(mat):
    size = len(mat)
    low = [[None] * size for _ in range(size)]
    for j in range(size):
        total = mat[j][j]
        for k in range(j):
            total = total - low[j][k] * low[j][k]
        low[j][j] = jnp.sqrt(total)
        for i in range(j + 1, size):
            total = mat[i][j]
            for k in range(j):
                total = total - low[i][k] * low[j][k]
            low[i][j] = total / low[j][j]
    return low


def cho_solve(low, inv_diag, rhs):
    size = len(low)
    half = []
    for i in range(size):
        total = rhs[i]
        for k in range(i):
            total = total - low[i][k] * half[k]
        half.append(total * inv_diag[i])
    out = [None] * size
    for i in reversed(range(size)):
        total = half[i]
        for k in range(i + 1, size):
            total = total - low[k][i] * out[k]
        out[i] = total * inv_diag[i]
    return out


def blur(cells, stride, coord, size):
    width = cells.shape[1]
    total = None
    for position in range(5):
        d = position - 2
        moved = cells if d == 0 else pltpu.roll(cells, (-d * stride) % width, 1)
        inside = (coord + d >= 0) & (coord + d < size)
        term = gauss_taps[position] * jnp.where(inside, moved, 0.0)
        total = term if total is None else total + term
    return total


def maps_kernel(
    n, m, per, freedom,
    x_hbm, cov_hbm, perm_hbm, mask_hbm, smooth_ref, peak_ref,
    raw, cov_ref, perm_ref, mask_ref, flat, shuf_a, shuf_b, des, des_all, designs,
    out_x, got_x, out, got, own, own_o, low, low_o, high, high_o, field, pk1, pk2,
    xsem, csem, xsend, xrecv, send, recv, hsend, hrecv, psend, prec, qsend, qrec,
):
    me = lax.axis_index("subj")
    slab = lax.axis_index("slab")
    plane = mask_ref.shape[1]
    copies = perm_ref.shape[0]
    rows = out.shape[2] - 8
    top = n * rows
    wide = out.shape[3]
    tiles = out.shape[0]
    blocks = perm_ref.shape[1] // BLOCK
    flat_rows = raw.shape[0] // perm_ref.shape[1]
    span = BLOCK * flat_rows

    small = [
        pltpu.make_async_copy(src, dst, csem.at[i])
        for i, (src, dst) in enumerate(((perm_hbm, perm_ref), (cov_hbm, cov_ref), (mask_hbm, mask_ref)))
    ]
    for copy in small:
        copy.start()

    def load(b):
        at = pl.ds(pl.multiple_of(b * span, span), span)
        return pltpu.make_async_copy(x_hbm.at[at], raw.at[at], xsem.at[b])

    def start_load(b, carry):
        load(b).start()
        return carry

    lax.fori_loop(0, blocks, start_load, 0)

    barrier = pltpu.get_barrier_semaphore()
    for o in range(1, n):
        pl.semaphore_signal(barrier, inc=1, device_id=(lax.rem(me + o, n), slab), device_id_type=MESH)
    for o in range(1, m):
        pl.semaphore_signal(barrier, inc=1, device_id=(me, lax.rem(slab + o, m)), device_id_type=MESH)

    shuf_a[...] = jnp.zeros_like(shuf_a)
    shuf_b[...] = jnp.zeros_like(shuf_b)
    des[...] = jnp.zeros_like(des)
    out_x[...] = jnp.zeros_like(out_x)
    for copy in small:
        copy.wait()

    row_high = lax.broadcasted_iota(jnp.int32, (8, BLOCK), 0) // 4
    one = jnp.ones((), jnp.bfloat16)
    zero = jnp.zeros((), jnp.bfloat16)

    def shuffle(b, carry):
        at = pl.ds(pl.multiple_of(b * BLOCK, BLOCK), BLOCK)
        place = (
            lax.broadcasted_iota(jnp.int32, (HALF // 16, 16, BLOCK), 0) * 16
            + lax.broadcasted_iota(jnp.int32, (HALF // 16, 16, BLOCK), 1)
        ).astype(jnp.float32).astype(jnp.bfloat16)
        cov = cov_ref[:, at].astype(jnp.float32)
        des[0:3, :] = cov
        des[4:7, :] = cov
        des[8:9, :] = cov[0:1]
        des[9:10, :] = jnp.ones((1, BLOCK), jnp.float32)
        des[10:12, :] = cov[1:3]
        shuf_a[top : top + 4, :] = des[8:12, 0:HALF]
        shuf_b[top : top + 4, :] = des[8:12, HALF:BLOCK]
        des_all[:, at] = des[8:24, :].astype(jnp.bfloat16)

        local = perm_ref[:, at] & (BLOCK - 1)
        upper = local // HALF
        lower = (local & (HALF - 1)).astype(jnp.float32)
        base = des[0:8, :]
        for pair in range(copies // 2):
            lefts = []
            hots = []
            for p in (2 * pair, 2 * pair + 1):
                lefts.append(jnp.where(upper[p : p + 1] == row_high, base, 0.0))
                spread = jnp.broadcast_to(lower[p : p + 1], (16, BLOCK)).astype(jnp.bfloat16)
                hots.append(jnp.where(spread[None] == place, one, zero).reshape(HALF, BLOCK))
            left = jnp.concatenate(lefts, axis=0).astype(jnp.bfloat16)
            hot = jnp.concatenate(hots, axis=0)
            moved = lax.dot_general(left, hot, NT, preferred_element_type=jnp.float32)
            for side in range(2):
                p = 2 * pair + side
                row = p // per * rows + p % per
                part = moved[8 * side : 8 * side + 8, HALF * side : HALF * side + HALF]
                shuf_a[pl.ds(row, 3, stride=per), :] = part[0:3]
                shuf_b[pl.ds(row, 3, stride=per), :] = part[4:7]
        designs[:, at] = jnp.concatenate([shuf_a[...], shuf_b[...]], axis=1).astype(jnp.bfloat16)

        load(b).wait()
        cells = pl.ds(pl.multiple_of(b * span, span), span)
        flat[cells, :] = raw[cells, :].astype(jnp.float32)
        return carry

    lax.fori_loop(0, blocks, shuffle, 0)

    crossed = lax.dot_general(designs[...], des_all[...], NT, preferred_element_type=jnp.float32)
    for g in range(n):
        out_x[g, 0:rows, 0:16] = crossed[g * rows : (g + 1) * rows]
        out_x[g, rows:, 0:16] = crossed[top : top + 8]

    pl.semaphore_wait(barrier, n + m - 2)

    def exchange(src, dst, send_sem, recv_sem):
        made = []
        for o in range(1, n):
            to = lax.rem(me + o, n)
            made.append(pltpu.make_async_remote_copy(
                src_ref=src(to), dst_ref=dst(o), send_sem=send_sem(o), recv_sem=recv_sem(o),
                device_id=(to, slab), device_id_type=MESH))
            made[-1].start()
        return made

    copies_x = exchange(
        lambda g: out_x.at[g], lambda o: got_x.at[o], lambda o: xsend.at[o], lambda o: xrecv.at[o])
    got_x[0] = out_x[me]

    group = min(4, blocks)
    depth_k = group * BLOCK
    sub = lax.broadcasted_iota(jnp.int32, (8, wide), 0)
    per_slice = tiles // 2
    copies_t = []
    for tile in range(tiles):
        first_row = [2 * (2 * (tile % per_slice) + i) + tile // per_slice for i in range(2)]

        def multiply(k, carry):
            acc, sq = carry
            start = pl.multiple_of(k * depth_k * flat_rows, depth_k * flat_rows)
            part = jnp.concatenate(
                [flat[pl.ds(start + r, depth_k, stride=flat_rows), :] for r in first_row], axis=1)
            at = pl.ds(pl.multiple_of(k * depth_k, depth_k), depth_k)
            acc = acc + jnp.dot(
                designs[:, at], part.astype(jnp.bfloat16), preferred_element_type=jnp.float32)
            sq = sq + jnp.sum((part * part).reshape(depth_k // 8, 8, wide), axis=0)
            return acc, sq

        acc, sq = lax.fori_loop(
            0, blocks // group, multiply,
            (jnp.zeros((designs.shape[0], wide), jnp.float32), jnp.zeros((8, wide), jnp.float32)))
        squares = jnp.sum(sq, axis=0, keepdims=True)
        seen_rows = jnp.where(sub == 4, squares, acc[top : top + 8])
        for g in range(n):
            out[tile, g, 0:rows, :] = acc[g * rows : (g + 1) * rows]
            out[tile, g, rows:, :] = seen_rows
        copies_t.append(exchange(
            lambda g: out.at[tile, g], lambda o: got.at[tile, o],
            lambda o: send.at[tile, o], lambda o: recv.at[tile, o]))
        got[tile, 0] = out[tile, me]

    cells = mask_ref[...].astype(jnp.float32)
    mask_row = jnp.concatenate([cells[0:1], cells[1:2]], axis=1)

    def source(s):
        return lax.rem(me - s + n, n)

    for copy in copies_x:
        copy.wait()
    seen_x = got_x[source(0), rows:]
    for s in range(1, n):
        seen_x = seen_x + got_x[source(s), rows:]
    mine_x = got_x[0, 0:rows]
    for o in range(1, n):
        mine_x = mine_x + got_x[o, 0:rows]
    gram = [[seen_x[i : i + 1, j : j + 1] for j in range(4)] for i in range(4)]
    low_z = cholesky([row[1:4] for row in gram[1:4]])
    inv_z = [1.0 / low_z[i][i] for i in range(3)]
    low_f = cholesky(gram)
    inv_diag = [1.0 / low_f[i][i] for i in range(4)]
    unit = [jnp.zeros((1, 1), jnp.float32), jnp.ones((1, 1), jnp.float32)]
    columns = [cho_solve(low_f, inv_diag, [unit[int(i == j)] for i in range(4)]) for j in range(4)]
    inverse = [[columns[j][i] for j in range(4)] for i in range(4)]

    for tile in range(tiles):
        for copy in copies_t[tile]:
            copy.wait()
        cols = slice(tile * wide, (tile + 1) * wide)
        obs = got[tile, source(0), rows:]
        for s in range(1, n):
            obs = obs + got[tile, source(s), rows:]
        chunk = got[tile, 0, 0:rows]
        for o in range(1, n):
            chunk = chunk + got[tile, o, 0:rows]
        prod = [obs[k : k + 1] for k in range(4)]
        fit = cho_solve(low_z, inv_z, prod[1:4])
        resid = obs[4:5] - (prod[1] * fit[0] + prod[2] * fit[1] + prod[3] * fit[2])

        def statistic(proj):
            slope = sum(inverse[0][k] * proj[k] for k in range(4))
            quad = sum(proj[k] * sum(inverse[k][l] * proj[l] for l in range(4)) for k in range(4))
            return slope / jnp.sqrt((resid - quad) / freedom * inverse[0][0])

        seen = [prod[k] - sum(gram[k][1 + i] * fit[i] for i in range(3)) for k in range(4)]
        own_o[:, cols] = statistic(seen) * mask_row[:, cols]
        proj = []
        for c in range(3):
            at = slice(c * per, (c + 1) * per)
            proj.append(chunk[at] - sum(mine_x[at, 1 + i : 2 + i] * fit[i] for i in range(3)))
        own[:, cols] = statistic([proj[0], seen[1], proj[1], proj[2]]) * mask_row[:, cols]

    up = (me, lax.rem(slab + 1, m))
    down = (me, lax.rem(slab + m - 1, m))

    def halo(src, dst, k, to):
        return pltpu.make_async_remote_copy(
            src_ref=src, dst_ref=dst, send_sem=hsend.at[k], recv_sem=hrecv.at[k],
            device_id=to, device_id_type=MESH)

    rise = [halo(own, low, 0, up), halo(own_o, low_o, 1, up)]
    fall = [halo(own, high, 2, down), halo(own_o, high_o, 3, down)]

    @pl.when(slab < m - 1)
    def _():
        for copy in rise:
            copy.start()

    @pl.when(slab > 0)
    def _():
        for copy in fall:
            copy.start()

    @pl.when(slab == 0)
    def _():
        low[...] = jnp.zeros_like(low)
        low_o[...] = jnp.zeros_like(low_o)

    @pl.when(slab == m - 1)
    def _():
        high[...] = jnp.zeros_like(high)
        high_o[...] = jnp.zeros_like(high_o)

    field[...] = jnp.zeros_like(field)

    @pl.when(slab > 0)
    def _():
        for copy in rise:
            copy.wait_recv()

    @pl.when(slab < m - 1)
    def _():
        for copy in fall:
            copy.wait_recv()

    def deep(lower, mine, upper):
        slices = []
        for ref in (lower, mine, upper):
            value = ref[...]
            slices += [value[:, :plane], value[:, plane:]]
        return [
            sum(gauss_taps[position] * slices[position + z] for position in range(5))
            for z in range(2)
        ]

    first, second = deep(low, own, high)
    field[0:per, :] = first
    field[8 : 8 + per, :] = second
    first, second = deep(low_o, own_o, high_o)
    field[16:17, :] = first
    field[17:18, :] = second

    cell = lax.broadcasted_iota(jnp.int32, (24, plane), 1)
    smooth = blur(field[...], PY, cell // PY, PX)
    smooth = blur(smooth, 1, cell % PY, PY)

    peaks = jnp.maximum(
        jnp.max(jnp.where(cells[0:1] > 0, smooth[0:per] * cells[0:1], -1e30), axis=1, keepdims=True),
        jnp.max(jnp.where(cells[1:2] > 0, smooth[8 : 8 + per] * cells[1:2], -1e30), axis=1, keepdims=True),
    )
    pk1[0] = jnp.broadcast_to(peaks, (per, LANES))
    copies_p = []
    for o in range(1, m):
        copies_p.append(pltpu.make_async_remote_copy(
            src_ref=pk1.at[0], dst_ref=pk1.at[o], send_sem=psend.at[o], recv_sem=prec.at[o],
            device_id=(me, lax.rem(slab + o, m)), device_id_type=MESH))
        copies_p[-1].start()
    seen_t = [smooth[16 + z : 17 + z] * cells[z : z + 1] for z in range(2)]
    smooth_ref[...] = jnp.concatenate(seen_t, axis=0)

    for copy in copies_p:
        copy.wait_recv()
    best = pk1[0]
    for o in range(1, m):
        best = jnp.maximum(best, pk1[o])
    pk2[0] = best
    copies_q = []
    for o in range(1, n):
        copies_q.append(pltpu.make_async_remote_copy(
            src_ref=pk2.at[0], dst_ref=pk2.at[o], send_sem=qsend.at[o], recv_sem=qrec.at[o],
            device_id=(lax.rem(me + o, n), slab), device_id_type=MESH))
        copies_q[-1].start()
    for copy in copies_q:
        copy.wait_recv()

    for o in range(n):
        peak_ref[lax.rem(me - o + n, n)] = pk2[o]

    for copy in copies_p + copies_q:
        copy.wait_send()

    @pl.when(slab < m - 1)
    def _():
        for copy in rise:
            copy.wait_send()

    @pl.when(slab > 0)
    def _():
        for copy in fall:
            copy.wait_send()


def p_kernel(smooth_ref, peaks_ref, mask_ref, t_ref, pval_ref, line_ref):
    n, per = peaks_ref.shape[:2]
    copies = n * per
    cells = mask_ref[...].astype(jnp.float32)
    values = smooth_ref[...]
    t_ref[...] = values
    line = jnp.zeros((1, LANES), jnp.float32)
    sub = lax.broadcasted_iota(jnp.int32, (per, LANES), 0)
    lane = lax.broadcasted_iota(jnp.int32, (per, LANES), 1)
    counts = [jnp.zeros((1, values.shape[1]), jnp.float32) for _ in range(2)]
    for d in range(n):
        value = peaks_ref[d]
        line = line + jnp.sum(jnp.where(lane == sub + d * per, value, 0.0), axis=0, keepdims=True)
        for z in range(2):
            level = jax.nn.sigmoid((value[:, 0:1] - values[z : z + 1]) / 0.2)
            counts[z] = counts[z] + jnp.sum(level, axis=0, keepdims=True)
    pval_ref[...] = cells * (1.0 + jnp.concatenate(counts, axis=0)) / (copies + 1)
    line_ref[...] = line[:, :copies]


def body(n, m, subjects_data, covariates, permutes, brain_mask):
    subj_rows, depth, plane = subjects_data.shape
    assert depth == 2 and plane == PX * PY
    copies = permutes.shape[0]
    per = copies // n
    rows = -(-3 * per // 8) * 8
    voxels = depth * plane
    wide = 2 * LANES
    tiles = voxels // wide
    lane_tiles = plane // LANES
    flat_rows = depth * lane_tiles
    data = (
        subjects_data.reshape(subj_rows, depth, lane_tiles, LANES)
        .transpose(0, 2, 1, 3)
        .reshape(subj_rows * flat_rows, LANES)
    )
    height = -(-(n * rows + 8) // 16) * 16
    f32 = jnp.float32
    bf16 = jnp.bfloat16
    vmem = pl.BlockSpec(memory_space=pltpu.VMEM)
    anywhere = pl.BlockSpec(memory_space=pl.ANY)
    dma = pltpu.SemaphoreType.DMA
    smooth, peaks = pl.pallas_call(
        functools.partial(maps_kernel, n, m, per, float(n * subj_rows - 4)),
        in_specs=[anywhere] * 4,
        out_specs=[vmem] * 2,
        out_shape=[
            jax.ShapeDtypeStruct((depth, plane), f32),
            jax.ShapeDtypeStruct((n, per, LANES), f32),
        ],
        scratch_shapes=[
            pltpu.VMEM((subj_rows * flat_rows, LANES), bf16),
            pltpu.VMEM((3, subj_rows), bf16),
            pltpu.VMEM((copies, subj_rows), jnp.int32),
            pltpu.VMEM((depth, plane), jnp.int32),
            pltpu.VMEM((subj_rows * flat_rows, LANES), f32),
            pltpu.VMEM((height, HALF), f32),
            pltpu.VMEM((height, HALF), f32),
            pltpu.VMEM((24, BLOCK), f32),
            pltpu.VMEM((16, subj_rows), bf16),
            pltpu.VMEM((height, subj_rows), bf16),
            pltpu.VMEM((n, rows + 8, LANES), f32),
            pltpu.VMEM((n, rows + 8, LANES), f32),
            pltpu.VMEM((tiles, n, rows + 8, wide), f32),
            pltpu.VMEM((tiles, n, rows + 8, wide), f32),
            pltpu.VMEM((per, voxels), f32),
            pltpu.VMEM((1, voxels), f32),
            pltpu.VMEM((per, voxels), f32),
            pltpu.VMEM((1, voxels), f32),
            pltpu.VMEM((per, voxels), f32),
            pltpu.VMEM((1, voxels), f32),
            pltpu.VMEM((24, plane), f32),
            pltpu.VMEM((m, per, LANES), f32),
            pltpu.VMEM((n, per, LANES), f32),
            dma((subj_rows // BLOCK,)), dma((3,)), dma((n,)), dma((n,)),
            dma((tiles, n)), dma((tiles, n)),
            dma((4,)), dma((4,)), dma((m,)), dma((m,)), dma((n,)), dma((n,)),
        ],
        compiler_params=pltpu.CompilerParams(
            collective_id=0, has_side_effects=True, vmem_limit_bytes=60 * 2**20
        ),
        name="maps",
    )(data, covariates, permutes, brain_mask)
    smooth_t, p_values, line = pl.pallas_call(
        p_kernel,
        in_specs=[vmem] * 3,
        out_specs=[vmem] * 3,
        out_shape=[
            jax.ShapeDtypeStruct((depth, plane), f32),
            jax.ShapeDtypeStruct((depth, plane), f32),
            jax.ShapeDtypeStruct((1, copies), f32),
        ],
        name="p_values",
    )(smooth, peaks, brain_mask)
    return smooth_t, p_values, line.reshape(copies)


def solution(mesh):
    return jax.shard_map(
        functools.partial(body, mesh.shape["subj"], mesh.shape["slab"]),
        mesh=mesh,
        in_specs=(P("subj", "slab", None), P(None, "subj"), P(None, "subj"), P("slab", None)),
        out_specs=(P("slab", None), P("slab", None), P()),
        check_vma=False,
    )
```

time: 45.4 us -> 38.8 us (0.85)
  local copies, waits for them, and re-layouts: 3.48 us -> 0 us
  Pallas kernels: 40.8 us -> 38 us
    unnamed x9 -> x0, local copies, waits for them, and re-layouts: 3.48 us -> none
    pallas_call x2, Pallas kernels: 40.8 us -> 38 us  [the longest x1 36.5 us: body(): pl.pallas_call(functools.partial(maps_kernel, n, m, per, float(n * subj_r...]
where the time goes in v2:
time: 38.8 us; the launch traced here: 38.6 us
  Pallas kernels  38 us (98%)
  between operations  0.64 us (2%)
    pallas_call x1, Pallas kernels, body(): pl.pallas_call(functools.partial(maps_kernel, n, m, per, float(n * subj_r...  36.5 us
    pallas_call x1, Pallas kernels, body(): pl.pallas_call(p_kernel, in_specs=[vmem] * 3, out_specs=[vmem] * 3, out_s...  1.44 us

profile of v2, /device:TPU:0, one launch (start us, length us, event | category | flops | bytes accessed | tf_op | source)
XLA Modules:
  0.0 38.6 jit_solution(5047278586760909594)
XLA Ops:
  0.6 36.5 %maps.1 = (f32[2,512]{1,0:T(2,128)}, f32[4,8,128]{2,1,0:T(8,128)}) custom-call(bf16[32768,128]{1,0:T(8,128)(2,1)} %bitcast.6, bf16[3,4096]{1,0:T(4,128)(2,1)} %cov_hbm.1, s32[32,4096]{1,0:T(8,128)} %perm_hbm.1, s32[2,512]{1,0:T(2,128)} %mask_ref.1), custom_call_target="tpu_custom_call" | custom-call | tf_op jit(solution)/shard_map/maps/pallas_call | solution.py:422
  37.2 1.4 %p_values.1 = (f32[2,512]{1,0:T(2,128)}, f32[2,512]{1,0:T(2,128)}, f32[1,32]{1,0:T(1,128)}) custom-call(f32[2,512]{1,0:T(2,128)} %get-tuple-element.8.smooth_ref, f32[4,8,128]{2,1,0:T(8,128)} %get-tuple-element.9.peaks_ref, s32[2,512]{1,0:T(2,128)} %mask_ref.1), custom_call_target="tpu_custom_call" | custom-call | tf_op jit(solution)/shard_map/p_values/pallas_call | solution.py:463

commit v3 on v2

--- a/solution.py
+++ b/solution.py
@@ -10,6 +10,7 @@
 
 BLOCK = 256
 HALF = 128
+QUARTER = 64
 PX = 16
 PY = 32
 LANES = 128
@@ -115,46 +116,54 @@
     for copy in small:
         copy.wait()
 
-    row_high = lax.broadcasted_iota(jnp.int32, (8, BLOCK), 0) // 4
+    row_high = lax.broadcasted_iota(jnp.int32, (16, BLOCK), 0) // 4
+    left_half = lax.broadcasted_iota(jnp.int32, (4, HALF), 1) < QUARTER
     one = jnp.ones((), jnp.bfloat16)
     zero = jnp.zeros((), jnp.bfloat16)
 
     def shuffle(b, carry):
         at = pl.ds(pl.multiple_of(b * BLOCK, BLOCK), BLOCK)
         place = (
-            lax.broadcasted_iota(jnp.int32, (HALF // 16, 16, BLOCK), 0) * 16
-            + lax.broadcasted_iota(jnp.int32, (HALF // 16, 16, BLOCK), 1)
+            lax.broadcasted_iota(jnp.int32, (QUARTER // 16, 16, BLOCK), 0) * 16
+            + lax.broadcasted_iota(jnp.int32, (QUARTER // 16, 16, BLOCK), 1)
         ).astype(jnp.float32).astype(jnp.bfloat16)
         cov = cov_ref[:, at].astype(jnp.float32)
-        des[0:3, :] = cov
-        des[4:7, :] = cov
-        des[8:9, :] = cov[0:1]
-        des[9:10, :] = jnp.ones((1, BLOCK), jnp.float32)
-        des[10:12, :] = cov[1:3]
-        shuf_a[top : top + 4, :] = des[8:12, 0:HALF]
-        shuf_b[top : top + 4, :] = des[8:12, HALF:BLOCK]
-        des_all[:, at] = des[8:24, :].astype(jnp.bfloat16)
+        for i in range(4):
+            des[4 * i : 4 * i + 3, :] = cov
+        des[16:17, :] = cov[0:1]
+        des[17:18, :] = jnp.ones((1, BLOCK), jnp.float32)
+        des[18:20, :] = cov[1:3]
+        shuf_a[top : top + 4, :] = des[16:20, 0:HALF]
+        shuf_b[top : top + 4, :] = des[16:20, HALF:BLOCK]
+        des_all[:, at] = des[16:32, :].astype(jnp.bfloat16)
 
         local = perm_ref[:, at] & (BLOCK - 1)
-        upper = local // HALF
-        lower = (local & (HALF - 1)).astype(jnp.float32)
-        base = des[0:8, :]
-        for pair in range(copies // 2):
+        upper = local // QUARTER
+        lower = (local & (QUARTER - 1)).astype(jnp.float32)
+        base = des[0:16, :]
+        for quad in range(copies // 4):
             lefts = []
             hots = []
-            for p in (2 * pair, 2 * pair + 1):
-                lefts.append(jnp.where(upper[p : p + 1] == row_high, base, 0.0))
+            for p in range(4 * quad, 4 * quad + 4):
+                lefts.append(jnp.where(upper[p : p + 1] == row_high, base, 0.0).astype(jnp.bfloat16))
                 spread = jnp.broadcast_to(lower[p : p + 1], (16, BLOCK)).astype(jnp.bfloat16)
-                hots.append(jnp.where(spread[None] == place, one, zero).reshape(HALF, BLOCK))
-            left = jnp.concatenate(lefts, axis=0).astype(jnp.bfloat16)
+                hots.append(jnp.where(spread[None] == place, one, zero).reshape(QUARTER, BLOCK))
+            left = jnp.concatenate(lefts, axis=0)
             hot = jnp.concatenate(hots, axis=0)
             moved = lax.dot_general(left, hot, NT, preferred_element_type=jnp.float32)
-            for side in range(2):
-                p = 2 * pair + side
+            for side in range(4):
+                p = 4 * quad + side
                 row = p // per * rows + p % per
-                part = moved[8 * side : 8 * side + 8, HALF * side : HALF * side + HALF]
-                shuf_a[pl.ds(row, 3, stride=per), :] = part[0:3]
-                shuf_b[pl.ds(row, 3, stride=per), :] = part[4:7]
+                tile_lanes = slice(HALF * (side // 2), HALF * (side // 2) + HALF)
+                for half, shuf in enumerate((shuf_a, shuf_b)):
+                    first = 16 * side + 8 * half
+                    part = moved[first : first + 8, tile_lanes]
+                    turned = pltpu.roll(part, QUARTER, 1)
+                    if side % 2 == 0:
+                        joined = jnp.where(left_half, part[0:4], turned[4:8])
+                    else:
+                        joined = jnp.where(left_half, turned[0:4], part[4:8])
+                    shuf[pl.ds(row, 3, stride=per), :] = joined[0:3]
         designs[:, at] = jnp.concatenate([shuf_a[...], shuf_b[...]], axis=1).astype(jnp.bfloat16)
 
         load(b).wait()
@@ -435,7 +444,7 @@
             pltpu.VMEM((subj_rows * flat_rows, LANES), f32),
             pltpu.VMEM((height, HALF), f32),
             pltpu.VMEM((height, HALF), f32),
-            pltpu.VMEM((24, BLOCK), f32),
+            pltpu.VMEM((32, BLOCK), f32),
             pltpu.VMEM((16, subj_rows), bf16),
             pltpu.VMEM((height, subj_rows), bf16),
             pltpu.VMEM((n, rows + 8, LANES), f32),

time: 38.8 us -> 36.6 us (0.943)
  Pallas kernels: 38 us -> 35.8 us
    pallas_call x1, Pallas kernels: 36.5 us -> 34.3 us  [body(): pl.pallas_call(functools.partial(maps_kernel, n, m, per, float(n * subj_r...]
where the time goes in v3:
time: 36.6 us; the launch traced here: 36.4 us
  Pallas kernels  35.8 us (98%)
  between operations  0.64 us (2%)
    pallas_call x1, Pallas kernels, body(): pl.pallas_call(functools.partial(maps_kernel, n, m, per, float(n * subj_r...  34.3 us
    pallas_call x1, Pallas kernels, body(): pl.pallas_call(p_kernel, in_specs=[vmem] * 3, out_specs=[vmem] * 3, out_s...  1.44 us

profile of v3, /device:TPU:0, one launch (start us, length us, event | category | flops | bytes accessed | tf_op | source)
XLA Modules:
  0.0 36.4 jit_solution(14097305805372367972)
XLA Ops:
  0.6 34.3 %maps.1 = (f32[2,512]{1,0:T(2,128)}, f32[4,8,128]{2,1,0:T(8,128)}) custom-call(bf16[32768,128]{1,0:T(8,128)(2,1)} %bitcast.6, bf16[3,4096]{1,0:T(4,128)(2,1)} %cov_hbm.1, s32[32,4096]{1,0:T(8,128)} %perm_hbm.1, s32[2,512]{1,0:T(2,128)} %mask_ref.1), custom_call_target="tpu_custom_call" | custom-call | tf_op jit(solution)/shard_map/maps/pallas_call | solution.py:431
  35.0 1.4 %p_values.1 = (f32[2,512]{1,0:T(2,128)}, f32[2,512]{1,0:T(2,128)}, f32[1,32]{1,0:T(1,128)}) custom-call(f32[2,512]{1,0:T(2,128)} %get-tuple-element.8.smooth_ref, f32[4,8,128]{2,1,0:T(8,128)} %get-tuple-element.9.peaks_ref, s32[2,512]{1,0:T(2,128)} %mask_ref.1), custom_call_target="tpu_custom_call" | custom-call | tf_op jit(solution)/shard_map/p_values/pallas_call | solution.py:472

commit v4 on v3

--- a/solution.py
+++ b/solution.py
@@ -71,8 +71,8 @@
     n, m, per, freedom,
     x_hbm, cov_hbm, perm_hbm, mask_hbm, smooth_ref, peak_ref,
     raw, cov_ref, perm_ref, mask_ref, flat, shuf_a, shuf_b, des, des_all, designs,
-    out_x, got_x, out, got, own, own_o, low, low_o, high, high_o, field, pk1, pk2,
-    xsem, csem, xsend, xrecv, send, recv, hsend, hrecv, psend, prec, qsend, qrec,
+    out_x, got_x, out, got, own, own_o, low, low_o, high, high_o, field, pk1,
+    xsem, csem, xsend, xrecv, send, recv, hsend, hrecv, psend, prec,
 ):
     me = lax.axis_index("subj")
     slab = lax.axis_index("slab")
@@ -104,10 +104,11 @@
     lax.fori_loop(0, blocks, start_load, 0)
 
     barrier = pltpu.get_barrier_semaphore()
-    for o in range(1, n):
-        pl.semaphore_signal(barrier, inc=1, device_id=(lax.rem(me + o, n), slab), device_id_type=MESH)
-    for o in range(1, m):
-        pl.semaphore_signal(barrier, inc=1, device_id=(me, lax.rem(slab + o, m)), device_id_type=MESH)
+    for a in range(n):
+        for o in range(m):
+            if a + o:
+                pl.semaphore_signal(
+                    barrier, inc=1, device_id=(lax.rem(me + a, n), lax.rem(slab + o, m)), device_id_type=MESH)
 
     shuf_a[...] = jnp.zeros_like(shuf_a)
     shuf_b[...] = jnp.zeros_like(shuf_b)
@@ -178,7 +179,7 @@
         out_x[g, 0:rows, 0:16] = crossed[g * rows : (g + 1) * rows]
         out_x[g, rows:, 0:16] = crossed[top : top + 8]
 
-    pl.semaphore_wait(barrier, n + m - 2)
+    pl.semaphore_wait(barrier, n * m - 1)
 
     def exchange(src, dst, send_sem, recv_sem):
         made = []
@@ -194,7 +195,7 @@
         lambda g: out_x.at[g], lambda o: got_x.at[o], lambda o: xsend.at[o], lambda o: xrecv.at[o])
     got_x[0] = out_x[me]
 
-    group = min(4, blocks)
+    group = min(8, blocks)
     depth_k = group * BLOCK
     sub = lax.broadcasted_iota(jnp.int32, (8, wide), 0)
     per_slice = tiles // 2
@@ -344,35 +345,28 @@
         jnp.max(jnp.where(cells[0:1] > 0, smooth[0:per] * cells[0:1], -1e30), axis=1, keepdims=True),
         jnp.max(jnp.where(cells[1:2] > 0, smooth[8 : 8 + per] * cells[1:2], -1e30), axis=1, keepdims=True),
     )
-    pk1[0] = jnp.broadcast_to(peaks, (per, LANES))
+    pk1[0, 0] = jnp.broadcast_to(peaks, (per, LANES))
     copies_p = []
-    for o in range(1, m):
-        copies_p.append(pltpu.make_async_remote_copy(
-            src_ref=pk1.at[0], dst_ref=pk1.at[o], send_sem=psend.at[o], recv_sem=prec.at[o],
-            device_id=(me, lax.rem(slab + o, m)), device_id_type=MESH))
-        copies_p[-1].start()
+    for a in range(n):
+        for o in range(m):
+            if a + o:
+                copies_p.append(pltpu.make_async_remote_copy(
+                    src_ref=pk1.at[0, 0], dst_ref=pk1.at[a, o],
+                    send_sem=psend.at[a, o], recv_sem=prec.at[a, o],
+                    device_id=(lax.rem(me + a, n), lax.rem(slab + o, m)), device_id_type=MESH))
+                copies_p[-1].start()
     seen_t = [smooth[16 + z : 17 + z] * cells[z : z + 1] for z in range(2)]
     smooth_ref[...] = jnp.concatenate(seen_t, axis=0)
 
     for copy in copies_p:
         copy.wait_recv()
-    best = pk1[0]
-    for o in range(1, m):
-        best = jnp.maximum(best, pk1[o])
-    pk2[0] = best
-    copies_q = []
-    for o in range(1, n):
-        copies_q.append(pltpu.make_async_remote_copy(
-            src_ref=pk2.at[0], dst_ref=pk2.at[o], send_sem=qsend.at[o], recv_sem=qrec.at[o],
-            device_id=(lax.rem(me + o, n), slab), device_id_type=MESH))
-        copies_q[-1].start()
-    for copy in copies_q:
-        copy.wait_recv()
-
-    for o in range(n):
-        peak_ref[lax.rem(me - o + n, n)] = pk2[o]
-
-    for copy in copies_p + copies_q:
+    for a in range(n):
+        best = pk1[a, 0]
+        for o in range(1, m):
+            best = jnp.maximum(best, pk1[a, o])
+        peak_ref[lax.rem(me - a + n, n)] = best
+
+    for copy in copies_p:
         copy.wait_send()
 
     @pl.when(slab < m - 1)
@@ -458,11 +452,10 @@
             pltpu.VMEM((per, voxels), f32),
             pltpu.VMEM((1, voxels), f32),
             pltpu.VMEM((24, plane), f32),
-            pltpu.VMEM((m, per, LANES), f32),
-            pltpu.VMEM((n, per, LANES), f32),
+            pltpu.VMEM((n, m, per, LANES), f32),
             dma((subj_rows // BLOCK,)), dma((3,)), dma((n,)), dma((n,)),
             dma((tiles, n)), dma((tiles, n)),
-            dma((4,)), dma((4,)), dma((m,)), dma((m,)), dma((n,)), dma((n,)),
+            dma((4,)), dma((4,)), dma((n, m)), dma((n, m)),
         ],
         compiler_params=pltpu.CompilerParams(
             collective_id=0, has_side_effects=True, vmem_limit_bytes=60 * 2**20

time: 36.6 us -> 35.3 us (0.964)
  Pallas kernels: 35.8 us -> 34.5 us
    pallas_call x1, Pallas kernels: 34.3 us -> 33 us  [body(): pl.pallas_call(functools.partial(maps_kernel, n, m, per, float(n * subj_r...]
where the time goes in v4:
time: 35.3 us; the launch traced here: 35.1 us
  Pallas kernels  34.5 us (98%)
  between operations  0.64 us (2%)
    pallas_call x1, Pallas kernels, body(): pl.pallas_call(functools.partial(maps_kernel, n, m, per, float(n * subj_r...  33 us
    pallas_call x1, Pallas kernels, body(): pl.pallas_call(p_kernel, in_specs=[vmem] * 3, out_specs=[vmem] * 3, out_s...  1.44 us

profile of v4, /device:TPU:0, one launch (start us, length us, event | category | flops | bytes accessed | tf_op | source)
XLA Modules:
  0.0 35.1 jit_solution(226361504339939664)
XLA Ops:
  0.6 33.0 %maps.1 = (f32[2,512]{1,0:T(2,128)}, f32[4,8,128]{2,1,0:T(8,128)}) custom-call(bf16[32768,128]{1,0:T(8,128)(2,1)} %bitcast.6, bf16[3,4096]{1,0:T(4,128)(2,1)} %cov_hbm.1, s32[32,4096]{1,0:T(8,128)} %perm_hbm.1, s32[2,512]{1,0:T(2,128)} %mask_ref.1), custom_call_target="tpu_custom_call" | custom-call | tf_op jit(solution)/shard_map/maps/pallas_call | solution.py:425
  33.7 1.4 %p_values.1 = (f32[2,512]{1,0:T(2,128)}, f32[2,512]{1,0:T(2,128)}, f32[1,32]{1,0:T(1,128)}) custom-call(f32[2,512]{1,0:T(2,128)} %get-tuple-element.8.smooth_ref, f32[4,8,128]{2,1,0:T(8,128)} %get-tuple-element.9.peaks_ref, s32[2,512]{1,0:T(2,128)} %mask_ref.1), custom_call_target="tpu_custom_call" | custom-call | tf_op jit(solution)/shard_map/p_values/pallas_call | solution.py:465
